TPU v7x, 128 devices: a whole 4x4x4 slice. The times are simulated.
128 devices in a mesh: blk: 16 (over z, y_lo, core), exp: 8 (over y_hi, x).
Axes of the slice: x: 4, y: 4 (y_hi: 2, y_lo: 2; y = y_hi * 2 + y_lo), z: 4, core: 2. Of those that a mesh axis runs over, the one named last changes fastest.
Arguments:
- nodes: bfloat16 [24576, 512], P('blk'), may hold values from -8 to 8
- attention_weights: bfloat16 [3, 256, 512], P(None, 'exp'), may hold values from -1.5 to 1.5
- output_weight: bfloat16 [256, 512], P('exp'), may hold values from -2 to 2
- router_weight: bfloat16 [8, 512], replicated, may hold values from -1.25 to 1.25
- gain_first: float32 [512], replicated, may hold values from 0.1 to 1.9
- gain_second: float32 [512], replicated, may hold values from 0.1 to 1.9
- expert_in: bfloat16 [8, 2048, 512], P('exp', 'blk'), may hold values from -0.25 to 0.25
- expert_out: bfloat16 [8, 2048, 512], P('exp', 'blk'), may hold values from -0.125 to 0.125
- routes: int32 [24576, 2], P(('blk', 'exp')), may hold values from 0 to 7, all different within a row; in each aligned block of 192 rows (0 to 191, 192 to 383, ...) at most 96 rows name the same one
- cotangent: bfloat16 [24576, 512], P(('blk', 'exp')), may hold values from -6 to 6
Outputs:
- layer_out: bfloat16 [24576, 512], P(('blk', 'exp'))
- stream_grad: bfloat16 [24576, 512], P(('blk', 'exp'))
- expert_in_grad: float32 [8, 2048, 512], P('exp', 'blk')
- expert_out_grad: float32 [8, 2048, 512], P('exp', 'blk')
- router_grad: float32 [8, 512], replicated
- gain_grad: float32 [512], replicated
Inputs may be any that keep to these rules, and one draw needn't show every extreme that they name: `routes`: each row names two different experts. Among the rows of one device (aligned blocks of 192 rows) no expert is named by more than 96 rows, and in some block one expert is named by exactly 96 rows.
All inputs are finite; a program needn't handle non-finite values.
Results may differ from a plain program's by a relative error of at most 0.04.
The roundings to bfloat16 on the way count: a program that leaves them out, or rounds other values in their place, can miss the bound.
Values may be sent and summed in bfloat16 or wider, within the bound.
No kernel may reach another device: no remote copies, remote signals or barrier semaphores. Data moves between devices by JAX's collectives and lax.ppermute only.
A program may use at most 64 MiB of HBM per device.

v0:
```python
import math
import jax
import jax.numpy as jnp
from jax import lax
from jax.sharding import PartitionSpec as P

HD = 32
EPSILON = 1e-06
NEG_LARGE = -1e30


def rms_gain(stream, gain):
    return stream * lax.rsqrt(jnp.mean(stream * stream, axis=-1, keepdims=True) + EPSILON) * gain


def gelu_tanh(values):
    return jax.nn.gelu(values, approximate=True)


def to_sources(buffer):
    return lax.all_to_all(buffer, "exp", split_axis=0, concat_axis=0, tiled=True)


def local(
    nodes,
    attention_weights,
    output_weight,
    router_weight,
    gain_first,
    gain_second,
    expert_in,
    expert_out,
    routes,
    cotangent,
):
    exp_count = lax.axis_size("exp")
    blk_count = lax.axis_size("blk")
    block_rows = nodes.shape[0]
    width = nodes.shape[1]
    features = attention_weights.shape[1]
    heads_here = features // HD
    own_rows = block_rows // exp_count
    capacity = 4 * block_rows // (exp_count * exp_count)
    experts = router_weight.shape[0]
    grad_scale = 1.0 / math.sqrt(block_rows * blk_count)
    score_scale = 1.0 / math.sqrt(HD)
    query = jnp.einsum(
        "td,fd->tf", nodes, attention_weights[0], preferred_element_type=jnp.float32
    ).astype(jnp.bfloat16)
    query_heads = query.reshape(block_rows, heads_here, HD).transpose(1, 0, 2)
    keys_values = jnp.einsum(
        "td,cfd->cft", nodes, attention_weights[1:], preferred_element_type=jnp.float32
    ).astype(jnp.bfloat16)
    start_state = (
        jnp.full((heads_here, block_rows), NEG_LARGE, jnp.float32),
        jnp.zeros((heads_here, block_rows), jnp.float32),
        jnp.zeros((heads_here, block_rows, HD), jnp.float32),
    )
    totals = start_state
    shard_piece = lax.all_gather(keys_values, "blk", axis=2, tiled=True)
    length = shard_piece.shape[2]
    key_width = math.gcd(length, 1024)
    key_blocks = shard_piece.reshape(2, heads_here, HD, length // key_width, key_width).transpose(
        3, 0, 1, 2, 4
    )

    def key_step(running, key_block):
        run_max, run_sum, accum = running
        scores = (
            jnp.einsum(
                "htf,hfk->htk", query_heads, key_block[0], preferred_element_type=jnp.float32
            )
            * score_scale
        )
        new_max = jnp.maximum(run_max, jnp.max(scores, axis=-1))
        shrink = jnp.exp(run_max - new_max)
        weights = jnp.exp(scores - new_max[..., None])
        run_sum = run_sum * shrink + jnp.sum(weights, axis=-1)
        update = jnp.einsum(
            "htk,hfk->htf",
            weights.astype(jnp.bfloat16),
            key_block[1],
            preferred_element_type=jnp.float32,
        )
        accum = accum * shrink[..., None] + update
        return ((new_max, run_sum, accum), None)

    totals, _ = lax.scan(key_step, totals, key_blocks)
    run_max, run_sum, accum = totals
    attended = (accum / run_sum[..., None]).astype(jnp.bfloat16)
    by_rows = attended.transpose(1, 0, 2).reshape(block_rows, features)
    attn_out = lax.psum_scatter(
        jnp.dot(by_rows, output_weight, preferred_element_type=jnp.float32).astype(jnp.bfloat16),
        "exp",
        scatter_dimension=0,
        tiled=True,
    ).astype(jnp.float32)
    own_nodes = lax.dynamic_slice_in_dim(
        nodes, lax.axis_index("exp") * own_rows, own_rows, 0
    ).astype(jnp.float32)
    stream = rms_gain(own_nodes + attn_out, gain_first).astype(jnp.bfloat16)
    logits = jnp.dot(stream, router_weight.T, preferred_element_type=jnp.float32)
    flat_routes = routes.reshape(2 * own_rows)
    choose = (flat_routes[:, None] == jnp.arange(experts, dtype=jnp.int32)[None, :]).astype(
        jnp.int32
    )
    before = jnp.cumsum(choose, axis=0) - choose
    slot_index = jnp.sum(before * choose, axis=1)
    position = flat_routes * capacity + slot_index
    dispatch_table = (
        jnp.arange(experts * capacity, dtype=jnp.int32)[:, None] == position[None, :]
    ).astype(jnp.bfloat16)
    selected = choose.reshape(own_rows, 2, experts).astype(jnp.float32)

    def gate_values(values):
        picked = jnp.sum(jax.nn.sigmoid(values)[:, None, :] * selected, axis=-1)
        return picked / jnp.sum(picked, axis=-1, keepdims=True)

    gates, gate_back = jax.vjp(gate_values, logits)
    repeated = jnp.repeat(stream, 2, axis=0)
    outgoing = jnp.dot(dispatch_table, repeated, preferred_element_type=jnp.float32).astype(
        jnp.bfloat16
    )
    outgoing = outgoing.reshape(experts, capacity, width)
    weight_rows_in, weight_rows_out = (
        lax.all_gather(expert_in[0], "blk", axis=0, tiled=True),
        lax.all_gather(expert_out[0], "blk", axis=0, tiled=True),
    )
    arrived = lax.all_to_all(outgoing, "exp", split_axis=0, concat_axis=0, tiled=True)
    pre_act = jnp.einsum("scd,hd->sch", arrived, weight_rows_in, preferred_element_type=jnp.float32)
    expert_hidden = gelu_tanh(pre_act).astype(jnp.bfloat16)
    result = jnp.einsum(
        "sch,hd->scd", expert_hidden, weight_rows_out, preferred_element_type=jnp.float32
    ).astype(jnp.bfloat16)
    received, pre_act, returned = (arrived, pre_act, to_sources(result))
    expert_rows = jnp.einsum(
        "ps,pd->sd",
        dispatch_table,
        returned.reshape(experts * capacity, width),
        preferred_element_type=jnp.float32,
    )
    expert_rows = expert_rows.reshape(own_rows, 2, width)
    mixture = gates[:, 0:1] * expert_rows[:, 0] + gates[:, 1:2] * expert_rows[:, 1]
    stream_two = stream.astype(jnp.float32) + mixture
    normed, norm_back = jax.vjp(rms_gain, stream_two, gain_second)
    layer_out = normed.astype(jnp.bfloat16)
    grad_two, gain_part = norm_back(cotangent.astype(jnp.float32))
    gate_grads = jnp.sum(expert_rows * grad_two[:, None, :], axis=-1)
    assigned_grads = (
        (gates[..., None] * grad_two[:, None, :]).astype(jnp.bfloat16).reshape(2 * own_rows, width)
    )
    grad_outgoing = jnp.dot(
        dispatch_table, assigned_grads, preferred_element_type=jnp.float32
    ).astype(jnp.bfloat16)
    grad_arrived = lax.all_to_all(
        grad_outgoing.reshape(experts, capacity, width),
        "exp",
        split_axis=0,
        concat_axis=0,
        tiled=True,
    )
    again_in, again_out = (
        lax.all_gather(expert_in[0], "blk", axis=0, tiled=True),
        lax.all_gather(expert_out[0], "blk", axis=0, tiled=True),
    )
    hidden_full, gelu_back = jax.vjp(gelu_tanh, pre_act)
    hidden = hidden_full.astype(jnp.bfloat16)
    hidden_grad = jnp.einsum(
        "scd,hd->sch", grad_arrived, again_out, preferred_element_type=jnp.float32
    )
    pre_grad = gelu_back(hidden_grad)[0].astype(jnp.bfloat16)
    term_in = jnp.einsum("sch,scd->hd", pre_grad, received, preferred_element_type=jnp.float32)
    term_out = jnp.einsum("sch,scd->hd", hidden, grad_arrived, preferred_element_type=jnp.float32)
    summed_grads = lax.psum_scatter(
        (jnp.concatenate([term_in, term_out], axis=1) * grad_scale).astype(jnp.bfloat16),
        "blk",
        scatter_dimension=0,
        tiled=True,
    ).astype(jnp.float32)
    expert_in_grad = summed_grads[None, :, :width]
    expert_out_grad = summed_grads[None, :, width:]
    rows_back = jnp.einsum(
        "sch,hd->scd", pre_grad, again_in, preferred_element_type=jnp.float32
    ).astype(jnp.bfloat16)
    back_home = to_sources(rows_back)
    back_rows = jnp.einsum(
        "ps,pd->sd",
        dispatch_table,
        back_home.reshape(experts * capacity, width),
        preferred_element_type=jnp.float32,
    )
    back_rows = back_rows.reshape(own_rows, 2, width)
    logit_grad = gate_back(gate_grads)[0]
    router_part = (
        jnp.dot(logit_grad.T, stream.astype(jnp.float32), precision=lax.Precision.HIGHEST)
        * grad_scale
    )
    router_grad, gain_grad = lax.psum((router_part, gain_part * grad_scale), ("blk", "exp"))
    router_term = jnp.dot(
        logit_grad, router_weight.astype(jnp.float32), precision=lax.Precision.HIGHEST
    )
    stream_grad = (grad_two + (back_rows[:, 0] + back_rows[:, 1]) + router_term).astype(
        jnp.bfloat16
    )
    return (layer_out, stream_grad, expert_in_grad, expert_out_grad, router_grad, gain_grad)


def solution(mesh):
    placed = (
        P("blk", None),
        P(None, "exp", None),
        P("exp", None),
        P(),
        P(),
        P(),
        P("exp", "blk", None),
        P("exp", "blk", None),
        P(("blk", "exp"), None),
        P(("blk", "exp"), None),
    )
    return jax.shard_map(
        local,
        mesh=mesh,
        in_specs=placed,
        out_specs=(
            P(("blk", "exp"), None),
            P(("blk", "exp"), None),
            P("exp", "blk", None),
            P("exp", "blk", None),
            P(),
            P(),
        ),
        check_vma=False,
    )
```

profile of v0, /device:TPU:1, one launch (start us, length us, event | category | flops | bytes accessed | tf_op | source)
XLA Modules:
  0.0 604.8 jit_solution(10231152198393182954)
XLA Ops:
  7.2 2.7 convolution_convert_fusion.1
  12.3 37.7 %all-gather.6.cloned.1.call-done = bf16[2,32,24576]{2,1,0:T(8,128)(2,1)} async-done(((bf16[2,32,1536]{2,1,0:T(8,128)(2,1)}), bf16[2,32,24576]{2,1,0:T(8,128)(2,1)}) %all-gather.6.cloned.1.call-update) | async-done | bytes 3145744 | tf_op jit(solution)/shard_map/all_gather | solution.py:60
  50.0 3.7 copy.60
  53.7 3.4 copy.66
  57.1 231.9 %while.15 = (s32[]{:T(128)}, f32[1,1536]{1,0:T(1,128)S(1)}, f32[1,1536]{1,0:T(1,128)S(1)}, f32[1,1536,32]{1,2,0:T(8,128)S(1)}, bf16[24,2,1,32,1024]{4,3,2,1,0:T(...) while((s32[]{:T(128)}, f32[1,1536]{1,0:T(1,128)S(1)}, ...), condition=%wide.region_3.4_spmd.clone, body=%wide.region_0.3_spmd.clone.sunk | while | flops 214066176 | bytes 44767396 | solution.py:88
  59.1 2.6 copy-done.1
  62.8 4.0 fusion.103
  68.8 2.6 copy-done.1
  72.5 4.0 fusion.103
  78.4 2.6 copy-done.1
  82.1 4.0 fusion.103
  88.1 2.6 copy-done.1
  91.8 4.0 fusion.103
  97.8 2.6 copy-done.1
  101.5 4.0 fusion.103
  107.4 2.6 copy-done.1
  111.1 4.0 fusion.103
  117.1 2.6 copy-done.1
  120.8 4.0 fusion.103
  126.7 2.6 copy-done.1
  130.5 4.0 fusion.103
  136.4 2.6 copy-done.1
  140.1 4.0 fusion.103
  146.1 2.6 copy-done.1
  149.8 4.0 fusion.103
  155.7 2.6 copy-done.1
  159.4 4.0 fusion.103
  165.4 2.6 copy-done.1
  169.1 4.0 fusion.103
  175.1 2.6 copy-done.1
  178.8 4.0 fusion.103
  184.7 2.6 copy-done.1
  188.4 4.0 fusion.103
  194.4 2.6 copy-done.1
  198.1 4.0 fusion.103
  204.0 2.6 copy-done.1
  207.8 4.0 fusion.103
  217.4 4.0 fusion.103
  227.1 4.0 fusion.103
  236.7 4.0 fusion.103
  246.4 4.0 fusion.103
  252.4 2.6 copy-done.1
  256.1 4.0 fusion.103
  262.0 2.6 copy-done.1
  265.7 4.0 fusion.103
  271.7 2.6 copy-done.1
  275.4 4.0 fusion.103
  285.1 4.0 fusion.103
  293.9 69.8 %reduce-scatter.5.cloned.1.call-done = bf16[192,512]{1,0:T(8,128)(2,1)} async-done(((bf16[1536,512]{1,0:T(8,128)(2,1)}), bf16[192,512]{1,0:T(8,128)(2,1)}) %reduce-scatter.5.cloned.1.call-update) | async-done | bytes 196624 | tf_op jit(solution)/shard_map/reduce_scatter | solution.py:92
  367.9 3.7 all-to-all-start
  373.0 32.2 %all-gather.8.cloned.1.call-done = bf16[1,2048,512]{2,1,0:T(8,128)(2,1)} async-done(((bf16[1,128,512]{2,1,0:T(8,128)(2,1)}), bf16[1,2048,512]{2,1,0:T(8,128)(2,1)}) %all-gather.8.cloned.1.call-update) | async-done | bytes 2097168 | tf_op jit(solution)/shard_map/all_gather | solution.py:126
  405.2 6.1 %fusion.32 = f32[8,96,2048]{2,1,0:T(8,128)} fusion(bf16[8,96,512]{2,1,0:T(8,128)(2,1)S(1)} %all-to-all-done, bf16[1,2048,512]{2,1,0:T(8,128)(2,1)} %all-gather.8.cloned.1.call-done), kind=kOutput, calls=%fused_computation.46 | convolution fusion | flops 1610612736 | bytes 9175040 | tf_op jit(solution)/shard_map/scd,hd->sch/dot_general | solution.py:130
  411.2 30.7 %all-gather.10.cloned.1.call-done = bf16[1,2048,512]{2,1,0:T(8,128)(2,1)} async-done(((bf16[1,128,512]{2,1,0:T(8,128)(2,1)}), bf16[1,2048,512]{2,1,0:T(8,128)(2,1)}) %all-gather.10.cloned.1.call-update) | async-done | bytes 2097168 | tf_op jit(solution)/shard_map/all_gather | solution.py:127
  441.9 6.5 %fusion.38 = bf16[8,96,512]{2,1,0:T(8,128)(2,1)} fusion(bf16[1,2048,512]{2,1,0:T(8,128)(2,1)} %all-gather.10.cloned.1.call-done, f32[8,96,2048]{2,1,0:T(8,128)} %fusion.32), kind=kOutput, calls=%fused_computation.50 | convolution fusion | flops 1625161728 | bytes 9175040 | tf_op jit(solution)/shard_map/sch,hd->scd/dot_general | solution.py:132
  448.4 5.9 all-to-all-start.1
  454.9 14.0 %all-to-all-done.1 = bf16[8,96,512]{2,1,0:T(8,128)(2,1)S(1)} async-done(((bf16[8,96,512]{2,1,0:T(8,128)(2,1)}), bf16[8,96,512]{2,1,0:T(8,128)(2,1)S(1)}, u32[]{:S(2)}, u32[]{:S(2)}) %all-to-all-start.1) | async-done | bytes 786464 | tf_op jit(solution)/shard_map/all_to_all | solution.py:21
  475.3 16.2 %all_to_all.20 = bf16[8,96,512]{2,1,0:T(8,128)(2,1)S(1)} all-to-all(bf16[8,96,512]{2,1,0:T(8,128)(2,1)S(1)} %bitcast.131), channel_id=1, replica_groups=mesh['blk'=16,'exp'=8] {'exp'}, dimensions={0} | all-to-all | bytes 1572864 | tf_op jit(solution)/shard_map/all_to_all | solution.py:155
  491.5 7.8 %fusion.25 = bf16[8,96,2048]{2,1,0:T(8,128)(2,1)S(1)} fusion(f32[8,96,2048]{2,1,0:T(8,128)} %fusion.32, bf16[8,96,512]{2,1,0:T(8,128)(2,1)S(1)} %all_to_all.20, bf16[1,2048,512]{2,1,0:T(8,128)(2,1)} %all-gather.10.cloned.1.call-done), kind=kOutput, calls=%fused_computation.32 | convolution fusion | flops 1642070016 | bytes 12320768 | tf_op jit(solution)/shard_map/scd,hd->sch/dot_general | solution.py:168
  499.3 2.9 convolution_bitcast_fusion
  504.1 2.6 fusion.18
  506.7 6.4 %copy.56 = bf16[2048,1024]{1,0:T(8,128)(2,1)} copy(bf16[2048,1024]{0,1:T(8,128)(2,1)} %fusion.18) | data formatting | bytes 8388608
  513.3 5.3 fusion.35
  518.6 3.5 all-to-all-start.3
  522.4 71.4 %all-reduce = (f32[8,512]{1,0:T(8,128)}, f32[512]{0:T(512)}) all-reduce(f32[8,512]{1,0:T(8,128)S(1)} %convolution_multiply_fusion, f32[512]{0:T(512)S(1)} %broadcast_multiply_fusion), channel_id=1, replica_groups=mesh['blk'=16,'exp'=8] {'blk','exp'}, use_global_device_ids=true, to_apply=%region_17.18 | all-reduce | flops 4608 | bytes 36864 | tf_op jit(solution)/shard_map/psum | solution.py:198
  (238 shorter events, 112.0 us)
Async XLA Ops:
  7.2 281.9 %copy-start = (bf16[32,512]{1,0:T(8,128)(2,1)S(1)}, bf16[32,512]{1,0:T(8,128)(2,1)}, u32[]{:S(2)}) copy-start(bf16[32,512]{1,0:T(8,128)(2,1)} %param.14) | copy-start | bytes 98308
  7.2 42.8 %all-gather.6.cloned.1.call-start = ((), (), s32[]{:S(2)}) async-start(), calls=%async_computation.6 | async-start | bytes 3342336 | tf_op jit(solution)/shard_map/all_gather | solution.py:60
  10.0 353.7 %reduce-scatter.5.cloned.1.call-start = ((), (), s32[]{:S(2)}) async-start(), calls=%async_computation.7 | async-start | bytes 1769472 | tf_op jit(solution)/shard_map/reduce_scatter | solution.py:92
  57.1 235.2 %copy-start.5 = (s32[192,2]{0,1:T(2,128)S(1)}, s32[192,2]{0,1:T(2,128)}, u32[]{:S(2)}) copy-start(s32[192,2]{0,1:T(2,128)} %param.20) | copy-start | bytes 4612
  57.1 307.8 %copy-start.7 = (f32[512]{0:T(512)S(1)}, f32[512]{0:T(512)}, u32[]{:S(2)}) copy-start(f32[512]{0:T(512)} %param.16) | copy-start | bytes 6148
  59.0 2.7 copy-start.1
  68.7 2.7 copy-start.1
  78.4 2.7 copy-start.1
  88.0 2.7 copy-start.1
  97.7 2.7 copy-start.1
  107.4 2.7 copy-start.1
  117.0 2.7 copy-start.1
  126.7 2.7 copy-start.1
  136.3 2.7 copy-start.1
  146.0 2.7 copy-start.1
  155.7 2.7 copy-start.1
  165.3 2.7 copy-start.1
  175.0 2.7 copy-start.1
  184.7 2.7 copy-start.1
  194.3 2.7 copy-start.1
  204.0 2.7 copy-start.1
  213.7 2.7 copy-start.1
  223.3 2.7 copy-start.1
  233.0 2.7 copy-start.1
  242.6 2.7 copy-start.1
  252.3 2.7 copy-start.1
  262.0 2.7 copy-start.1
  271.6 2.7 copy-start.1
  281.3 2.7 copy-start.1
  291.0 114.2 %all-gather.8.cloned.1.call-start = ((), (), s32[]{:S(2)}) async-start(), calls=%async_computation.8 | async-start | bytes 2228224 | tf_op jit(solution)/shard_map/all_gather | solution.py:126
  291.7 150.2 %all-gather.10.cloned.1.call-start = ((), (), s32[]{:S(2)}) async-start(), calls=%async_computation.9 | async-start | bytes 2228224 | tf_op jit(solution)/shard_map/all_gather | solution.py:127
  367.9 37.2 %all-to-all-start = ((bf16[8,96,512]{2,1,0:T(8,128)(2,1)}), bf16[8,96,512]{2,1,0:T(8,128)(2,1)S(1)}, u32[]{:S(2)}, u32[]{:S(2)}) async-start(bf16[8,96,512]{2,1,0:T(8,128)(2,1)} %bitcast.8), calls=%async_computation.1 | async-start | bytes 1572864 | tf_op jit(solution)/shard_map/all_to_all | solution.py:129
  411.2 43.1 %copy-start.4 = (bf16[8,512]{1,0:T(8,128)(2,1)S(1)}, bf16[8,512]{1,0:T(8,128)(2,1)}, u32[]{:S(2)}) copy-start(bf16[8,512]{1,0:T(8,128)(2,1)} %param.15) | copy-start | bytes 24580
  411.2 59.4 %copy-start.2 = (bf16[192,512]{1,0:T(8,128)(2,1)S(1)}, bf16[192,512]{1,0:T(8,128)(2,1)}, u32[]{:S(2)}) copy-start(bf16[192,512]{1,0:T(8,128)(2,1)} %param.21) | copy-start | bytes 589828
  411.2 59.4 %copy-start.6 = (f32[512]{0:T(512)S(1)}, f32[512]{0:T(512)}, u32[]{:S(2)}) copy-start(f32[512]{0:T(512)} %param.17) | copy-start | bytes 6148
  448.4 20.5 %all-to-all-start.1 = ((bf16[8,96,512]{2,1,0:T(8,128)(2,1)}), bf16[8,96,512]{2,1,0:T(8,128)(2,1)S(1)}, u32[]{:S(2)}, u32[]{:S(2)}) async-start(bf16[8,96,512]{2,1,0:T(8,128)(2,1)} %fusion.38), calls=%async_computation.2 | async-start | bytes 1572864 | tf_op jit(solution)/shard_map/all_to_all | solution.py:21
  454.3 141.1 %reduce-scatter.7.cloned.1.call-start = ((), (), s32[]{:S(2)}) async-start(), calls=%async_computation.10 | async-start | bytes 4456448
  475.3 24.0 %slice-start = ((s8[6291456]{0:T(1024)(128)(4,1)}), s8[4194304]{0:T(1024)(128)(4,1)S(1)}, s32[]{:S(2)}) async-start(s8[6291456]{0:T(1024)(128)(4,1)} %bitcast.127), calls=%async_computation.11 | async-start | bytes 8388608
  491.5 7.8 %slice-start.1 = ((s8[6291456]{0:T(1024)(128)(4,1)}), s8[2097152]{0:T(1024)(128)(4,1)S(1)}, s32[]{:S(2)}) async-start(s8[6291456]{0:T(1024)(128)(4,1)} %bitcast.127), calls=%async_computation.12 | async-start | bytes 4194304
  499.3 2.9 copy-start.8
  513.3 80.5 %copy-start.3 = (pred[192,2,768]{2,1,0:T(4,128)(4,1)S(1)}, pred[192,2,768]{2,1,0:T(4,128)(4,1)}, u32[]{:S(2)}) copy-start(pred[192,2,768]{2,1,0:T(4,128)(4,1)} %eq.74) | copy-start | bytes 884740
  518.6 75.2 %all-to-all-start.3 = ((bf16[8,96,512]{2,1,0:T(8,128)(2,1)}), bf16[8,96,512]{2,1,0:T(8,128)(2,1)S(1)}, u32[]{:S(2)}, u32[]{:S(2)}) async-start(bf16[8,96,512]{2,1,0:T(8,128)(2,1)} %fusion.35), calls=%async_computation.4 | async-start | bytes 1572864 | tf_op jit(solution)/shard_map/all_to_all | solution.py:21
Sparse Core Ops, SparseCore 0:
  10.2 39.6 all-gather.5
  291.1 72.5 reduce-scatter.4
  365.4 39.6 all-gather.7
  406.7 35.1 all-gather.9
  513.2 72.5 reduce-scatter.6
where the time goes:
time: 607 us; the launch traced here: 605 us
  waiting for transfers between devices  186 us (31%)
  matrix products  183 us (30%)
  blocking collectives  87.7 us (14%)
  local copies, waits for them, and re-layouts  84.3 us (14%)
  other arithmetic  35.3 us (6%)
  between operations  14.2 us (2%)
  starting transfers between devices  13.4 us (2%)
    dot_general x24, matrix products, key_step(): jnp.einsum('htk,hfk->htf', weights.astype(jnp.bfloat16), key_block[1], pr...  95.5 us
    psum x1, blocking collectives, local(): lax.psum((router_part, gain_part * grad_scale), ('blk', 'exp'))  71.4 us
    reduce_scatter x1, waiting for transfers between devices, local(): lax.psum_scatter(jnp.dot(by_rows, output_weight, preferred_element_type=j...  69.8 us
    while x72, local copies, waits for them, and re-layouts  62.5 us
    dot_general x24, matrix products, key_step(): jnp.einsum('htf,hfk->htk', query_heads, key_block[0], preferred_element_t...  45.2 us
    all_gather x1, waiting for transfers between devices, local(): shard_piece = lax.all_gather(keys_values, 'blk', axis=2, tiled=True)  37.7 us
    all_gather x1, waiting for transfers between devices, local(): lax.all_gather(expert_in[0], 'blk', axis=0, tiled=True)  32.2 us
    all_gather x1, waiting for transfers between devices, local(): lax.all_gather(expert_out[0], 'blk', axis=0, tiled=True)  30.7 us
  transfers between devices with their start and end apart: 8, of which 5 were waited for; matrix products, arithmetic and copies ran while one was open for 4% of the time, Pallas kernels for 0%

commit v1 on v0

--- a/solution.py
+++ b/solution.py
@@ -195,7 +195,7 @@
         jnp.dot(logit_grad.T, stream.astype(jnp.float32), precision=lax.Precision.HIGHEST)
         * grad_scale
     )
-    router_grad, gain_grad = lax.psum((router_part, gain_part * grad_scale), ("blk", "exp"))
+    router_grad, gain_grad = lax.psum(lax.psum((router_part, gain_part * grad_scale), "exp"), "blk")
     router_term = jnp.dot(
         logit_grad, router_weight.astype(jnp.float32), precision=lax.Precision.HIGHEST
     )

time: 607 us -> 632 us (1.041)
  blocking collectives: 87.7 us -> 110 us
    psum x1 -> x2, blocking collectives: 71.4 us -> 93.7 us  [the longest x1 56.7 us: local(): lax.psum(lax.psum((router_part, gain_part * grad_scale), 'exp'), 'blk')]
where the time goes in v1:
time: 632 us; the launch traced here: 627 us
  waiting for transfers between devices  186 us (29%)
  matrix products  183 us (29%)
  blocking collectives  110 us (17%)
  local copies, waits for them, and re-layouts  84.3 us (13%)
  other arithmetic  35.3 us (6%)
  between operations  14.2 us (2%)
  starting transfers between devices  13.4 us (2%)
    dot_general x24, matrix products, key_step(): jnp.einsum('htk,hfk->htf', weights.astype(jnp.bfloat16), key_block[1], pr...  95.5 us
    reduce_scatter x1, waiting for transfers between devices, local(): lax.psum_scatter(jnp.dot(by_rows, output_weight, preferred_element_type=j...  69.8 us
    while x72, local copies, waits for them, and re-layouts  62.5 us
    psum x1, blocking collectives, local(): lax.psum(lax.psum((router_part, gain_part * grad_scale), 'exp'), 'blk')  56.7 us
    dot_general x24, matrix products, key_step(): jnp.einsum('htf,hfk->htk', query_heads, key_block[0], preferred_element_t...  45.2 us
    all_gather x1, waiting for transfers between devices, local(): shard_piece = lax.all_gather(keys_values, 'blk', axis=2, tiled=True)  37.7 us
    psum x1, blocking collectives, local(): lax.psum((router_part, gain_part * grad_scale), 'exp')  37 us
    all_gather x1, waiting for transfers between devices, local(): lax.all_gather(expert_in[0], 'blk', axis=0, tiled=True)  32.2 us
  transfers between devices with their start and end apart: 8, of which 5 were waited for; matrix products, arithmetic and copies ran while one was open for 4% of the time, Pallas kernels for 0%

profile of v1, /device:TPU:1, one launch (start us, length us, event | category | flops | bytes accessed | tf_op | source)
XLA Modules:
  0.0 627.0 jit_solution(125966703579476056)
XLA Ops:
  7.2 2.7 convolution_convert_fusion.1
  12.3 37.7 %all-gather.6.cloned.1.call-done = bf16[2,32,24576]{2,1,0:T(8,128)(2,1)} async-done(((bf16[2,32,1536]{2,1,0:T(8,128)(2,1)}), bf16[2,32,24576]{2,1,0:T(8,128)(2,1)}) %all-gather.6.cloned.1.call-update) | async-done | bytes 3145744 | tf_op jit(solution)/shard_map/all_gather | solution.py:60
  50.0 3.7 copy.60
  53.7 3.4 copy.66
  57.1 231.9 %while.15 = (s32[]{:T(128)}, f32[1,1536]{1,0:T(1,128)S(1)}, f32[1,1536]{1,0:T(1,128)S(1)}, f32[1,1536,32]{1,2,0:T(8,128)S(1)}, bf16[24,2,1,32,1024]{4,3,2,1,0:T(...) while((s32[]{:T(128)}, f32[1,1536]{1,0:T(1,128)S(1)}, ...), condition=%wide.region_3.4_spmd.clone, body=%wide.region_0.3_spmd.clone.sunk | while | flops 214066176 | bytes 44767396 | solution.py:88
  59.1 2.6 copy-done.1
  62.8 4.0 fusion.103
  68.8 2.6 copy-done.1
  72.5 4.0 fusion.103
  78.4 2.6 copy-done.1
  82.1 4.0 fusion.103
  88.1 2.6 copy-done.1
  91.8 4.0 fusion.103
  97.8 2.6 copy-done.1
  101.5 4.0 fusion.103
  107.4 2.6 copy-done.1
  111.1 4.0 fusion.103
  117.1 2.6 copy-done.1
  120.8 4.0 fusion.103
  126.7 2.6 copy-done.1
  130.5 4.0 fusion.103
  136.4 2.6 copy-done.1
  140.1 4.0 fusion.103
  146.1 2.6 copy-done.1
  149.8 4.0 fusion.103
  155.7 2.6 copy-done.1
  159.4 4.0 fusion.103
  165.4 2.6 copy-done.1
  169.1 4.0 fusion.103
  175.1 2.6 copy-done.1
  178.8 4.0 fusion.103
  184.7 2.6 copy-done.1
  188.4 4.0 fusion.103
  194.4 2.6 copy-done.1
  198.1 4.0 fusion.103
  207.8 4.0 fusion.103
  217.4 4.0 fusion.103
  227.1 4.0 fusion.103
  236.7 4.0 fusion.103
  246.4 4.0 fusion.103
  252.4 2.6 copy-done.1
  256.1 4.0 fusion.103
  262.0 2.6 copy-done.1
  265.7 4.0 fusion.103
  271.7 2.6 copy-done.1
  275.4 4.0 fusion.103
  285.1 4.0 fusion.103
  293.9 69.8 %reduce-scatter.5.cloned.1.call-done = bf16[192,512]{1,0:T(8,128)(2,1)} async-done(((bf16[1536,512]{1,0:T(8,128)(2,1)}), bf16[192,512]{1,0:T(8,128)(2,1)}) %reduce-scatter.5.cloned.1.call-update) | async-done | bytes 196624 | tf_op jit(solution)/shard_map/reduce_scatter | solution.py:92
  367.9 3.7 all-to-all-start
  373.0 32.2 %all-gather.8.cloned.1.call-done = bf16[1,2048,512]{2,1,0:T(8,128)(2,1)} async-done(((bf16[1,128,512]{2,1,0:T(8,128)(2,1)}), bf16[1,2048,512]{2,1,0:T(8,128)(2,1)}) %all-gather.8.cloned.1.call-update) | async-done | bytes 2097168 | tf_op jit(solution)/shard_map/all_gather | solution.py:126
  405.2 6.1 fusion.32
  411.2 30.7 %all-gather.10.cloned.1.call-done = bf16[1,2048,512]{2,1,0:T(8,128)(2,1)} async-done(((bf16[1,128,512]{2,1,0:T(8,128)(2,1)}), bf16[1,2048,512]{2,1,0:T(8,128)(2,1)}) %all-gather.10.cloned.1.call-update) | async-done | bytes 2097168 | tf_op jit(solution)/shard_map/all_gather | solution.py:127
  441.9 6.5 %fusion.38 = bf16[8,96,512]{2,1,0:T(8,128)(2,1)} fusion(bf16[1,2048,512]{2,1,0:T(8,128)(2,1)} %all-gather.10.cloned.1.call-done, f32[8,96,2048]{2,1,0:T(8,128)} %fusion.32), kind=kOutput, calls=%fused_computation.50 | convolution fusion | flops 1625161728 | bytes 9175040 | tf_op jit(solution)/shard_map/sch,hd->scd/dot_general | solution.py:132
  448.4 5.9 all-to-all-start.1
  454.9 14.0 %all-to-all-done.1 = bf16[8,96,512]{2,1,0:T(8,128)(2,1)S(1)} async-done(((bf16[8,96,512]{2,1,0:T(8,128)(2,1)}), bf16[8,96,512]{2,1,0:T(8,128)(2,1)S(1)}, u32[]{:S(2)}, u32[]{:S(2)}) %all-to-all-start.1) | async-done | bytes 786464 | tf_op jit(solution)/shard_map/all_to_all | solution.py:21
  475.3 16.2 %all_to_all.20 = bf16[8,96,512]{2,1,0:T(8,128)(2,1)S(1)} all-to-all(bf16[8,96,512]{2,1,0:T(8,128)(2,1)S(1)} %bitcast.131), channel_id=1, replica_groups=mesh['blk'=16,'exp'=8] {'exp'}, dimensions={0} | all-to-all | bytes 1572864 | tf_op jit(solution)/shard_map/all_to_all | solution.py:155
  491.5 7.8 %fusion.25 = bf16[8,96,2048]{2,1,0:T(8,128)(2,1)S(1)} fusion(f32[8,96,2048]{2,1,0:T(8,128)} %fusion.32, bf16[8,96,512]{2,1,0:T(8,128)(2,1)S(1)} %all_to_all.20, bf16[1,2048,512]{2,1,0:T(8,128)(2,1)} %all-gather.10.cloned.1.call-done), kind=kOutput, calls=%fused_computation.32 | convolution fusion | flops 1642070016 | bytes 12320768 | tf_op jit(solution)/shard_map/scd,hd->sch/dot_general | solution.py:168
  499.3 2.9 convolution_bitcast_fusion
  504.1 2.6 fusion.18
  506.7 6.4 %copy.56 = bf16[2048,1024]{1,0:T(8,128)(2,1)} copy(bf16[2048,1024]{0,1:T(8,128)(2,1)} %fusion.18) | data formatting | bytes 8388608
  513.3 5.3 fusion.35
  518.6 3.5 all-to-all-start.3
  522.4 37.0 %all-reduce.1 = (f32[8,512]{1,0:T(8,128)S(1)}, f32[512]{0:T(512)S(1)}) all-reduce(f32[8,512]{1,0:T(8,128)S(1)} %convolution_multiply_fusion, f32[512]{0:T(512)S(1)} %broadcast_multiply_fusion), channel_id=1, replica_groups=mesh['blk'=16,'exp'=8] {'exp'}, use_global_device_ids=true, to_apply=%region_17.18 | all-reduce | flops 4608 | bytes 36864 | tf_op jit(solution)/shard_map/psum | solution.py:198
  559.4 56.7 %all-reduce = (f32[8,512]{1,0:T(8,128)}, f32[512]{0:T(512)}) all-reduce(f32[8,512]{1,0:T(8,128)S(1)} %get-tuple-element.130, f32[512]{0:T(512)S(1)} %get-tuple-element.131), channel_id=1, replica_groups=mesh['blk'=16,'exp'=8] {'blk'}, use_global_device_ids=true, to_apply=%region_18.19 | all-reduce | flops 4608 | bytes 36864 | tf_op jit(solution)/shard_map/psum | solution.py:198
  (239 shorter events, 114.6 us)
Async XLA Ops:
  7.2 281.9 %copy-start = (bf16[32,512]{1,0:T(8,128)(2,1)S(1)}, bf16[32,512]{1,0:T(8,128)(2,1)}, u32[]{:S(2)}) copy-start(bf16[32,512]{1,0:T(8,128)(2,1)} %param.14) | copy-start | bytes 98308
  7.2 42.8 %all-gather.6.cloned.1.call-start = ((), (), s32[]{:S(2)}) async-start(), calls=%async_computation.6 | async-start | bytes 3342336 | tf_op jit(solution)/shard_map/all_gather | solution.py:60
  10.0 353.7 %reduce-scatter.5.cloned.1.call-start = ((), (), s32[]{:S(2)}) async-start(), calls=%async_computation.7 | async-start | bytes 1769472 | tf_op jit(solution)/shard_map/reduce_scatter | solution.py:92
  57.1 235.2 %copy-start.5 = (s32[192,2]{0,1:T(2,128)S(1)}, s32[192,2]{0,1:T(2,128)}, u32[]{:S(2)}) copy-start(s32[192,2]{0,1:T(2,128)} %param.20) | copy-start | bytes 4612
  57.1 307.8 %copy-start.7 = (f32[512]{0:T(512)S(1)}, f32[512]{0:T(512)}, u32[]{:S(2)}) copy-start(f32[512]{0:T(512)} %param.16) | copy-start | bytes 6148
  59.0 2.7 copy-start.1
  68.7 2.7 copy-start.1
  78.4 2.7 copy-start.1
  88.0 2.7 copy-start.1
  97.7 2.7 copy-start.1
  107.4 2.7 copy-start.1
  117.0 2.7 copy-start.1
  126.7 2.7 copy-start.1
  136.3 2.7 copy-start.1
  146.0 2.7 copy-start.1
  155.7 2.7 copy-start.1
  165.3 2.7 copy-start.1
  175.0 2.7 copy-start.1
  184.7 2.7 copy-start.1
  194.3 2.7 copy-start.1
  204.0 2.7 copy-start.1
  213.7 2.7 copy-start.1
  223.3 2.7 copy-start.1
  233.0 2.7 copy-start.1
  242.6 2.7 copy-start.1
  252.3 2.7 copy-start.1
  262.0 2.7 copy-start.1
  271.6 2.7 copy-start.1
  281.3 2.7 copy-start.1
  291.0 114.2 %all-gather.8.cloned.1.call-start = ((), (), s32[]{:S(2)}) async-start(), calls=%async_computation.8 | async-start | bytes 2228224 | tf_op jit(solution)/shard_map/all_gather | solution.py:126
  291.7 150.2 %all-gather.10.cloned.1.call-start = ((), (), s32[]{:S(2)}) async-start(), calls=%async_computation.9 | async-start | bytes 2228224 | tf_op jit(solution)/shard_map/all_gather | solution.py:127
  367.9 37.2 %all-to-all-start = ((bf16[8,96,512]{2,1,0:T(8,128)(2,1)}), bf16[8,96,512]{2,1,0:T(8,128)(2,1)S(1)}, u32[]{:S(2)}, u32[]{:S(2)}) async-start(bf16[8,96,512]{2,1,0:T(8,128)(2,1)} %bitcast.8), calls=%async_computation.1 | async-start | bytes 1572864 | tf_op jit(solution)/shard_map/all_to_all | solution.py:129
  411.2 43.1 %copy-start.4 = (bf16[8,512]{1,0:T(8,128)(2,1)S(1)}, bf16[8,512]{1,0:T(8,128)(2,1)}, u32[]{:S(2)}) copy-start(bf16[8,512]{1,0:T(8,128)(2,1)} %param.15) | copy-start | bytes 24580
  411.2 59.4 %copy-start.2 = (bf16[192,512]{1,0:T(8,128)(2,1)S(1)}, bf16[192,512]{1,0:T(8,128)(2,1)}, u32[]{:S(2)}) copy-start(bf16[192,512]{1,0:T(8,128)(2,1)} %param.21) | copy-start | bytes 589828
  411.2 59.4 %copy-start.6 = (f32[512]{0:T(512)S(1)}, f32[512]{0:T(512)}, u32[]{:S(2)}) copy-start(f32[512]{0:T(512)} %param.17) | copy-start | bytes 6148
  448.4 20.5 %all-to-all-start.1 = ((bf16[8,96,512]{2,1,0:T(8,128)(2,1)}), bf16[8,96,512]{2,1,0:T(8,128)(2,1)S(1)}, u32[]{:S(2)}, u32[]{:S(2)}) async-start(bf16[8,96,512]{2,1,0:T(8,128)(2,1)} %fusion.38), calls=%async_computation.2 | async-start | bytes 1572864 | tf_op jit(solution)/shard_map/all_to_all | solution.py:21
  454.3 163.3 %reduce-scatter.7.cloned.1.call-start = ((), (), s32[]{:S(2)}) async-start(), calls=%async_computation.10 | async-start | bytes 4456448
  475.3 24.0 %slice-start = ((s8[6291456]{0:T(1024)(128)(4,1)}), s8[4194304]{0:T(1024)(128)(4,1)S(1)}, s32[]{:S(2)}) async-start(s8[6291456]{0:T(1024)(128)(4,1)} %bitcast.127), calls=%async_computation.11 | async-start | bytes 8388608
  491.5 7.8 %slice-start.1 = ((s8[6291456]{0:T(1024)(128)(4,1)}), s8[2097152]{0:T(1024)(128)(4,1)S(1)}, s32[]{:S(2)}) async-start(s8[6291456]{0:T(1024)(128)(4,1)} %bitcast.127), calls=%async_computation.12 | async-start | bytes 4194304
  499.3 2.9 copy-start.8
  513.3 102.7 %copy-start.3 = (pred[192,2,768]{2,1,0:T(4,128)(4,1)S(1)}, pred[192,2,768]{2,1,0:T(4,128)(4,1)}, u32[]{:S(2)}) copy-start(pred[192,2,768]{2,1,0:T(4,128)(4,1)} %eq.74) | copy-start | bytes 884740
  518.6 97.5 %all-to-all-start.3 = ((bf16[8,96,512]{2,1,0:T(8,128)(2,1)}), bf16[8,96,512]{2,1,0:T(8,128)(2,1)S(1)}, u32[]{:S(2)}, u32[]{:S(2)}) async-start(bf16[8,96,512]{2,1,0:T(8,128)(2,1)} %fusion.35), calls=%async_computation.4 | async-start | bytes 1572864 | tf_op jit(solution)/shard_map/all_to_all | solution.py:21
Sparse Core Ops, SparseCore 0:
  10.2 39.6 all-gather.5
  291.1 72.5 reduce-scatter.4
  365.4 39.6 all-gather.7
  406.7 35.1 all-gather.9
  513.2 72.3 reduce-scatter.6
